TPU v7x, 256 devices: a whole 4x4x8 slice. The times are simulated.
256 devices in a mesh: wide: 32 (over y, x, core), batch: 8 (over z).
Axes of the slice: x: 4, y: 4, z: 8, core: 2. Of those that a mesh axis runs over, the one named last changes fastest.
Arguments:
- q_latent: bfloat16 [8, 64, 4, 1536], P('batch', 'wide'), may hold values from -6 to 6
- draft_start: int32 [8, 64], P('batch', 'wide'), may hold values from 4096 to 8191
- cache_len: int32 [8, 64], P('batch', 'wide'), may hold values from 1 to 4092, 163680 in all within a row
- latent_cache: bfloat16 [8, 64, 4096, 576], P('batch', 'wide'), may hold values from -576 to 576
- w_q_up: bfloat16 [1536, 24576], P('batch', 'wide'), may hold values from -0.15625 to 0.15625
- w_k_absorb: bfloat16 [128, 128, 512], P('wide'), may hold values from -0.5 to 0.5
- value_up_weight: bfloat16 [128, 512, 128], P('wide'), may hold values from -0.25 to 0.25
Outputs:
- values: bfloat16 [8, 64, 4, 16384], P('batch', None, None, 'wide')
All inputs are finite; a program needn't handle non-finite values. No bound on the sum of `cache_len` on one device may be relied on, other than what follows from the above.
Results may differ from a plain program's by a relative error of at most 0.014.
The roundings to bfloat16 on the way count: a program that leaves them out, or rounds other values in their place, can miss the bound.
Values may be sent and summed in bfloat16 or wider, within the bound.
No kernel may reach another device: no remote copies, remote signals or barrier semaphores. Data moves between devices by JAX's collectives and lax.ppermute only.
A program may use at most 128 MiB of HBM per device.

v0:
```python
import functools
import math

import jax
import jax.numpy as jnp
from jax import lax
from jax.experimental import pallas as pl
from jax.experimental.pallas import tpu as pltpu
from jax.sharding import PartitionSpec as P


BF16 = jnp.bfloat16
F32 = jnp.float32
VMEM_LIMIT = 58 << 20
LANES = 128
BLOCK = 2048


def near(x):
    return pltpu.with_memory_space_constraint(x, pltpu.VMEM)


def ring_gather(block, axis_name, size):
    up = [(i, (i + 1) % size) for i in range(size)]
    down = [(i, (i - 1) % size) for i in range(size)]
    half = size // 2
    middle = block.shape[0] // 2
    ahead = behind = block
    pieces = [((0, 0), block)]
    for step in range(1, half + 1):
        last = step == half
        ahead = lax.ppermute(ahead[:middle] if last else ahead, axis_name, up)
        behind = lax.ppermute(behind[middle:] if last else behind, axis_name, down)
        pieces += [((size - step, 0), ahead), ((step, middle if last else 0), behind)]
    return pieces


def query_kernel(layout, heads, nope, rope, owned, me_ref, q_ref, absorb_ref, *refs):
    *piece_refs, out_ref, w_ref, stage_ref = refs
    me = me_ref[0]
    senders, local_rows, depth = q_ref.shape
    rows = senders * local_rows
    width = nope + rope
    kv = absorb_ref.shape[2]
    parts = kv // LANES
    size = piece_refs[0].shape[0]
    for (back, row), piece in zip(layout, piece_refs):
        start = pl.multiple_of(lax.rem(me + back, depth // size) * size + row, 32)
        w_ref[pl.ds(start, piece.shape[0]), :] = piece[...]
    full = jnp.dot(q_ref[...].reshape(rows, depth), w_ref[...], preferred_element_type=F32)
    full = full.astype(BF16).astype(F32)
    for head in range(heads):
        start = head * width
        low = full[:, start : start + nope].astype(BF16)
        absorbed = jnp.dot(low, absorb_ref[head], preferred_element_type=F32)
        tail = full[:, start + nope : start + width]
        for g in range(parts):
            stage_ref[g, pl.ds(head, rows, stride=heads), :] = absorbed[
                :, g * LANES : (g + 1) * LANES
            ]
        stage_ref[parts, pl.ds(head, rows, stride=heads), :] = jnp.concatenate(
            [tail] * owned, axis=1
        )
    each = local_rows * heads
    group = each // owned
    for g in range(parts):
        out_ref[:, g * each : (g + 1) * each, :] = (
            stage_ref[g].astype(BF16).reshape(senders, each, LANES)
        )
    tails = stage_ref[parts].reshape(senders, owned, group, LANES)
    lane = lax.broadcasted_iota(jnp.int32, (senders, group, LANES), 2)
    out_ref[:, parts * each :, :] = jnp.where(lane < rope, tails[:, 0], tails[:, 1]).astype(BF16)


def build_query(me, q_all, pieces, absorb, rope, owned):
    layout = tuple(place for place, _ in pieces)
    flat = [piece for _, piece in pieces]
    heads, nope, kv = absorb.shape
    senders, local_rows, depth = q_all.shape
    rows = senders * local_rows
    vmem = pl.BlockSpec(memory_space=pltpu.VMEM)
    out_rows = local_rows * heads * (kv + rope) // LANES
    return pl.pallas_call(
        functools.partial(query_kernel, layout, heads, nope, rope, owned),
        out_shape=jax.ShapeDtypeStruct((senders, out_rows, LANES), BF16),
        in_specs=[pl.BlockSpec(memory_space=pltpu.SMEM)] + [vmem] * (2 + len(flat)),
        out_specs=vmem,
        scratch_shapes=[
            pltpu.VMEM((depth, flat[0].shape[1]), BF16),
            pltpu.VMEM((kv // LANES + 1, rows * heads, LANES), F32),
        ],
        compiler_params=pltpu.CompilerParams(vmem_limit_bytes=VMEM_LIMIT),
        name="build_query",
    )(me, near(q_all), absorb, *[near(piece) for piece in flat])


def attend_kernel(heads, drafts, kv, rope, factor, len_ref, q_ref, cos_ref, sin_ref, cache_ref, out_ref, *scratch):
    key_ref, qm_ref, score_ref, peak_ref, sum_ref, acc_ref, sem = scratch
    senders = q_ref.shape[0]
    owned, _, slots = key_ref.shape
    group = heads * drafts
    rows = senders * group
    blocks = slots // BLOCK
    parts = kv // LANES
    half = rope // 2

    def copy_of(r, b):
        span = pl.ds(b * BLOCK, BLOCK)
        return pltpu.make_async_copy(
            cache_ref.at[0, r, :, span], key_ref.at[r, :, span], sem.at[r, b]
        )

    limits = []
    for r in range(owned):
        length = len_ref[0, r]
        total = jnp.minimum((length + drafts - 1) // BLOCK + 1, blocks)
        limits.append((length, (length + 1) // BLOCK, total))
        for b in range(blocks):

            @pl.when(b < limits[r][2])
            def _():
                copy_of(r, b).start()

    for r in range(owned):
        length, full_blocks, total = limits[r]
        for g in range(parts):
            first = (g * owned + r) * group
            qm_ref[:, g * LANES : (g + 1) * LANES] = q_ref[:, first : first + group, :].reshape(
                rows, LANES
            )
        tail = q_ref[:, parts * owned * group :, r * rope : (r + 1) * rope].astype(F32)
        swapped = jnp.concatenate([tail[..., half:], tail[..., :half]], axis=-1)
        turned = tail * cos_ref[r] + swapped * sin_ref[r]
        qm_ref[:, kv:] = turned.astype(BF16).reshape(rows, rope)
        peak_ref[...] = jnp.full(peak_ref.shape, -jnp.inf, F32)
        sum_ref[...] = jnp.zeros(sum_ref.shape, F32)
        acc_ref[...] = jnp.zeros(acc_ref.shape, F32)

        def score_block(b, masked):
            copy_of(r, b).wait()
            start = pl.multiple_of(b * BLOCK, BLOCK)
            scores = jnp.dot(
                qm_ref[...], key_ref[r, :, pl.ds(start, BLOCK)], preferred_element_type=F32
            )
            if masked:
                slot = start + lax.broadcasted_iota(jnp.int32, scores.shape, 1)
                row = lax.broadcasted_iota(jnp.int32, scores.shape, 0)
                draft = lax.rem(row, group) // heads
                scores = jnp.where(slot <= length + draft, scores, -jnp.inf)
            score_ref[:, pl.ds(start, BLOCK)] = scores
            best = peak_ref[...]
            for g in range(BLOCK // LANES):
                best = jnp.maximum(best, scores[:, g * LANES : (g + 1) * LANES])
            peak_ref[...] = best

        def plain(b, carry):
            score_block(b, False)
            return carry

        def edge(b, carry):
            score_block(b, True)
            return carry

        lax.fori_loop(0, full_blocks, plain, 0)
        lax.fori_loop(full_blocks, total, edge, 0)
        peak = jnp.max(peak_ref[...], axis=1, keepdims=True) * factor

        def mix_block(b, carry):
            start = pl.multiple_of(b * BLOCK, BLOCK)
            weights = jnp.exp2(score_ref[:, pl.ds(start, BLOCK)] * factor - peak)
            partial = sum_ref[...]
            for g in range(BLOCK // LANES):
                partial = partial + weights[:, g * LANES : (g + 1) * LANES]
            sum_ref[...] = partial
            acc_ref[...] += lax.dot_general(
                weights.astype(BF16),
                key_ref[r, :kv, pl.ds(start, BLOCK)],
                (((1,), (1,)), ((), ())),
                preferred_element_type=F32,
            )
            return carry

        lax.fori_loop(0, total, mix_block, 0)
        norm = jnp.sum(sum_ref[...], axis=1, keepdims=True)
        out_ref[:, r * group : (r + 1) * group, :] = (
            (acc_ref[...] / norm).astype(BF16).reshape(senders, group, kv)
        )


def attend(arrived, cosine, sine, cache, lengths, heads, drafts, kv, rope, scale):
    senders = arrived.shape[0]
    owned, width, slots = cache.shape[1:]
    group = heads * drafts
    rows = senders * group
    vmem = pl.BlockSpec(memory_space=pltpu.VMEM)
    return pl.pallas_call(
        functools.partial(attend_kernel, heads, drafts, kv, rope, scale * math.log2(math.e)),
        out_shape=jax.ShapeDtypeStruct((senders, owned * group, kv), BF16),
        in_specs=[
            pl.BlockSpec(memory_space=pltpu.SMEM),
            vmem,
            vmem,
            vmem,
            pl.BlockSpec(memory_space=pl.ANY),
        ],
        out_specs=vmem,
        scratch_shapes=[
            pltpu.VMEM((owned, width, slots), BF16),
            pltpu.VMEM((rows, width), BF16),
            pltpu.VMEM((rows, slots), F32),
            pltpu.VMEM((rows, LANES), F32),
            pltpu.VMEM((rows, LANES), F32),
            pltpu.VMEM((rows, kv), F32),
            pltpu.SemaphoreType.DMA((owned, slots // BLOCK)),
        ],
        compiler_params=pltpu.CompilerParams(vmem_limit_bytes=VMEM_LIMIT),
        name="attend",
    )(lengths, near(arrived), cosine, sine, cache)


def value_kernel(lat_ref, up_ref, out_ref, stage_ref):
    parts, all_rows, _ = stage_ref.shape
    heads, _, width = up_ref.shape
    rows = all_rows // heads
    for g in range(parts):
        stage_ref[g] = lat_ref[..., g * LANES : (g + 1) * LANES].astype(F32).reshape(all_rows, LANES)
    for head in range(heads):
        low = [stage_ref[g, pl.ds(head, rows, stride=heads), :].astype(BF16) for g in range(parts)]
        low = jnp.concatenate(low, axis=1)
        value = jnp.dot(low, up_ref[head], preferred_element_type=F32)
        out_ref[:, :, head * width : (head + 1) * width] = value.reshape(
            out_ref.shape[0], out_ref.shape[1], width
        ).astype(BF16)


def expand_values(latent, up, drafts):
    heads, kv, width = up.shape
    rows = latent.shape[0] * latent.shape[1]
    vmem = pl.BlockSpec(memory_space=pltpu.VMEM)
    return pl.pallas_call(
        value_kernel,
        out_shape=jax.ShapeDtypeStruct((rows // (heads * drafts), drafts, heads * width), BF16),
        in_specs=[vmem, vmem],
        out_specs=vmem,
        scratch_shapes=[pltpu.VMEM((kv // LANES, rows, LANES), F32)],
        compiler_params=pltpu.CompilerParams(vmem_limit_bytes=VMEM_LIMIT),
        name="expand_values",
    )(near(latent), up)


def per_device(
    wide, batch, q_latent, draft_start, cache_len, latent_cache, w_q_up, w_k_absorb, value_up_weight
):
    heads_here, nope_width, kv_width = w_k_absorb.shape
    head_dim = w_q_up.shape[1] // heads_here
    rope_width = head_dim - nope_width
    scale = float(head_dim) ** (-0.5)
    _, owned, drafts, latent = q_latent.shape
    me = lax.axis_index("batch").astype(jnp.int32).reshape(1)

    pieces = ring_gather(w_q_up, "batch", batch)
    copies = jnp.broadcast_to(
        q_latent.reshape(1, owned * drafts, latent), (wide, owned * drafts, latent)
    )
    q_all = lax.all_to_all(copies, "wide", split_axis=0, concat_axis=0, tiled=True)
    query = build_query(me, q_all, pieces, w_k_absorb, rope_width, owned)
    arrived = lax.all_to_all(query, "wide", split_axis=0, concat_axis=0, tiled=True)

    half = rope_width // 2
    shape = (owned, drafts * heads_here, rope_width)
    lane = lax.broadcasted_iota(jnp.int32, shape, 2)
    draft = lax.broadcasted_iota(jnp.int32, shape, 1) // heads_here
    freqs = 10000.0 ** (-lax.rem(lane, half).astype(F32) * 2.0 / rope_width)
    angles = (draft_start[0][:, None, None] + draft).astype(F32) * freqs
    cosine = jnp.cos(angles)
    sine = jnp.sin(angles) * jnp.where(lane < half, -1.0, 1.0)

    mixed = attend(
        arrived,
        cosine,
        sine,
        jnp.swapaxes(latent_cache, 2, 3),
        cache_len,
        heads_here,
        drafts,
        kv_width,
        rope_width,
        scale,
    )
    returned = lax.all_to_all(mixed, "wide", split_axis=0, concat_axis=0, tiled=True)
    values = expand_values(returned, value_up_weight, drafts)
    return values.reshape(1, wide * owned, drafts, values.shape[2])


def solution(mesh):
    in_specs = (
        P("batch", "wide", None, None),
        P("batch", "wide"),
        P("batch", "wide"),
        P("batch", "wide", None, None),
        P("batch", "wide"),
        P("wide", None, None),
        P("wide", None, None),
    )
    out_specs = P("batch", None, None, "wide")
    return jax.shard_map(
        functools.partial(per_device, mesh.shape["wide"], mesh.shape["batch"]),
        mesh=mesh,
        in_specs=in_specs,
        out_specs=out_specs,
        check_vma=False,
    )
```

profile of v0, /device:TPU:1, one launch (start us, length us, event | category | flops | bytes accessed | tf_op | source)
XLA Modules:
  0.0 112.2 jit_solution(4490941628265154842)
XLA Ops:
  0.0 2.5 %collective-permute-start = (bf16[192,768]{1,0:T(8,128)(2,1)}, bf16[192,768]{1,0:T(8,128)(2,1)S(1)}, u32[]{:S(2)}, u32[]{:S(2)}) collective-permute-start(bf16[192,768]{1,0:T(8,128)(2,1)} %refs_0_.1), channel_id=1, source_target_pairs={{0,1},{1,2},{2,3},{3,4},{4,5},{5,6},{6,7},{7,0},{8,9},{9,10},{10,1... | collective-permute-start | bytes 884744 | tf_op jit(solution)/shard_map/ppermute | solution.py:32
  2.5 3.9 %collective-permute-start.1 = (bf16[192,768]{1,0:T(8,128)(2,1)}, bf16[192,768]{1,0:T(8,128)(2,1)S(1)}, u32[]{:S(2)}, u32[]{:S(2)}) collective-permute-start(bf16[192,768]{1,0:T(8,128)(2,1)} %refs_0_.1), channel_id=1, source_target_pairs={{0,7},{1,0},{2,1},{3,2},{4,3},{5,4},{6,5},{7,6},{8,15},{9,8},{10,9... | collective-permute-start | bytes 884744 | tf_op jit(solution)/shard_map/ppermute | solution.py:33
  6.4 0.7 broadcast_in_dim.15
  7.1 1.0 broadcast_in_dim.16
  8.1 0.0 copy-start
  8.1 8.2 %all-to-all-start = ((bf16[32,8,1536]{2,1,0:T(8,128)(2,1)}), bf16[32,8,1536]{2,1,0:T(8,128)(2,1)S(1)}, u32[]{:S(2)}, u32[]{:S(2)}) async-start(bf16[32,8,1536]{2,1,0:T(8,128)(2,1)} %broadcast_in_dim.16), calls=%async_computation | async-start | bytes 1572864 | tf_op jit(solution)/shard_map/all_to_all | solution.py:265
  16.3 0.0 collective-permute-done.refs_1_
  16.3 0.1 collective-permute-start.2
  16.4 0.0 collective-permute-done.1.refs_2_
  16.4 2.7 %collective-permute-start.3 = (bf16[192,768]{1,0:T(8,128)(2,1)S(1)}, bf16[192,768]{1,0:T(8,128)(2,1)S(1)}, u32[]{:S(2)}, u32[]{:S(2)}) collective-permute-start(bf16[192,768]{1,0:T(8,128)(2,1)S(1)} %collective-permute-done.1.refs_2_), channel_id=1, source_target_pairs={{0,7},{1,0},{2,1},{3,2},{4,3},{5,4},{6,5},{7,6},{8,15},{9,8},{10,9... | collective-permute-start | bytes 884744 | tf_op jit(solution)/shard_map/ppermute | solution.py:33
  19.1 6.9 %collective-permute-done.2.refs_3_ = bf16[192,768]{1,0:T(8,128)(2,1)S(1)} collective-permute-done((bf16[192,768]{1,0:T(8,128)(2,1)S(1)}, bf16[192,768]{1,0:T(8,128)(2,1)S(1)}, u32[]{:S(2)}, u32[]{:S(2)}) %collective-permute-start.2) | collective-permute-done | bytes 294944 | tf_op jit(solution)/shard_map/ppermute | solution.py:32
  25.9 0.0 collective-permute-start.4
  25.9 0.0 collective-permute-done.3.refs_4_
  25.9 2.7 %collective-permute-start.5 = (bf16[192,768]{1,0:T(8,128)(2,1)S(1)}, bf16[192,768]{1,0:T(8,128)(2,1)S(1)}, u32[]{:S(2)}, u32[]{:S(2)}) collective-permute-start(bf16[192,768]{1,0:T(8,128)(2,1)S(1)} %collective-permute-done.3.refs_4_), channel_id=1, source_target_pairs={{0,7},{1,0},{2,1},{3,2},{4,3},{5,4},{6,5},{7,6},{8,15},{9,8},{10,9... | collective-permute-start | bytes 884744 | tf_op jit(solution)/shard_map/ppermute | solution.py:33
  28.6 6.0 %collective-permute-done.4.refs_5_ = bf16[192,768]{1,0:T(8,128)(2,1)S(1)} collective-permute-done((bf16[192,768]{1,0:T(8,128)(2,1)S(1)}, bf16[192,768]{1,0:T(8,128)(2,1)S(1)}, u32[]{:S(2)}, u32[]{:S(2)}) %collective-permute-start.4) | collective-permute-done | bytes 294944 | tf_op jit(solution)/shard_map/ppermute | solution.py:32
  34.6 0.1 collective-permute-start.6
  34.7 0.0 collective-permute-done.5.refs_6_
  34.7 2.7 %collective-permute-start.7 = (bf16[96,768]{1,0:T(8,128)(2,1)S(1)}, bf16[96,768]{1,0:T(8,128)(2,1)S(1)}, u32[]{:S(2)}, u32[]{:S(2)}) collective-permute-start(bf16[96,768]{1,0:T(8,128)(2,1)S(1)} %slice.9), channel_id=1, source_target_pairs={{0,7},{1,0},{2,1},{3,2},{4,3},{5,4},{6,5},{7,6},{8,15},{9,8},{10,9... | collective-permute-start | bytes 442376 | tf_op jit(solution)/shard_map/ppermute | solution.py:33
  37.5 0.0 all-to-all-done.q_ref
  37.5 2.4 %collective-permute-done.6.refs_7_ = bf16[96,768]{1,0:T(8,128)(2,1)S(1)} collective-permute-done((bf16[96,768]{1,0:T(8,128)(2,1)S(1)}, bf16[96,768]{1,0:T(8,128)(2,1)S(1)}, u32[]{:S(2)}, u32[]{:S(2)}) %collective-permute-start.6) | collective-permute-done | bytes 147488 | tf_op jit(solution)/shard_map/ppermute | solution.py:32
  39.9 0.0 collective-permute-done.7.refs_8_
  39.9 0.0 copy-done
  39.9 3.6 %build_query.1 = bf16[32,144,128]{2,1,0:T(8,128)(2,1)} custom-call(s32[1]{0:T(128)} %bitcast.me_ref, bf16[32,8,1536]{2,1,0:T(8,128)(2,1)S(1)} %all-to-all-done.q_ref, bf16[4,128,512]{2,1,0:T(8,128)(2,1)} %absorb_ref.1, bf16[192,768]{1,0:T(8,128)(2,1)S(1)} %copy-done, bf16[192,768]{1,0:T(8,128)(2,1)S(1)} %collective-permute-done.refs_1_, ...), custom_call_target="tpu_custom_call" | custom-call | tf_op jit(solution)/shard_map/build_query/pallas_call | solution.py:83
  43.5 0.0 copy-start.1
  43.5 10.1 %all-to-all-start.1 = ((bf16[32,144,128]{2,1,0:T(8,128)(2,1)}), bf16[32,144,128]{2,1,0:T(8,128)(2,1)S(1)}, u32[]{:S(2)}, u32[]{:S(2)}) async-start(bf16[32,144,128]{2,1,0:T(8,128)(2,1)} %build_query.1), calls=%async_computation.1 | async-start | bytes 2359296 | tf_op jit(solution)/shard_map/all_to_all | solution.py:267
  53.6 0.0 copy-done.1
  53.6 0.8 sine_multiply_fusion
  54.4 17.7 %all-to-all-done.1.q_ref = bf16[32,144,128]{2,1,0:T(8,128)(2,1)S(1)} async-done(((bf16[32,144,128]{2,1,0:T(8,128)(2,1)}), bf16[32,144,128]{2,1,0:T(8,128)(2,1)S(1)}, u32[]{:S(2)}, u32[]{:S(2)}) %all-to-all-start.1) | async-done | bytes 1179680 | tf_op jit(solution)/shard_map/all_to_all | solution.py:267
  72.1 17.1 %attend.1 = bf16[32,32,512]{2,1,0:T(8,128)(2,1)} custom-call(s32[1,2]{1,0:T(1,128)} %len_ref.1, bf16[32,144,128]{2,1,0:T(8,128)(2,1)S(1)} %all-to-all-done.1.q_ref, f32[2,16,64]{2,1,0:T(8,128)} %get-tuple-element.6.cos_ref, f32[2,16,64]{2,1,0:T(8,128)} %get-tuple-element.5.sin_ref, bf16[1,2,576,4096]{3,2,1,0:T(8,128)(2,1)} %bitcast.4), custom_call_target="tpu_custom_call" | custom-call | tf_op jit(solution)/shard_map/attend/pallas_call | solution.py:196
  89.2 20.8 %all_to_all.15.lat_ref = bf16[32,32,512]{2,1,0:T(8,128)(2,1)S(1)} all-to-all(bf16[32,32,512]{2,1,0:T(8,128)(2,1)} %attend.1), channel_id=1, replica_groups=mesh['wide'=32,'batch'=8] {'wide'}, dimensions={0} | all-to-all | bytes 2097152 | tf_op jit(solution)/shard_map/all_to_all | solution.py:290
  109.9 2.2 %expand_values.1 = bf16[64,4,512]{2,1,0:T(4,128)(2,1)} custom-call(bf16[32,32,512]{2,1,0:T(8,128)(2,1)S(1)} %all_to_all.15.lat_ref, bf16[4,512,128]{2,1,0:T(8,128)(2,1)} %up_ref.1), custom_call_target="tpu_custom_call" | custom-call | tf_op jit(solution)/shard_map/expand_values/pallas_call | solution.py:240
  (5 shorter events, 0.0 us)
Async XLA Ops:
  0.0 16.3 %collective-permute-start = (bf16[192,768]{1,0:T(8,128)(2,1)}, bf16[192,768]{1,0:T(8,128)(2,1)S(1)}, u32[]{:S(2)}, u32[]{:S(2)}) collective-permute-start(bf16[192,768]{1,0:T(8,128)(2,1)} %refs_0_.1), channel_id=1, source_target_pairs={{0,1},{1,2},{2,3},{3,4},{4,5},{5,6},{6,7},{7,0},{8,9},{9,10},{10,1... | collective-permute-start | bytes 884744 | tf_op jit(solution)/shard_map/ppermute | solution.py:32
  2.5 13.9 %collective-permute-start.1 = (bf16[192,768]{1,0:T(8,128)(2,1)}, bf16[192,768]{1,0:T(8,128)(2,1)S(1)}, u32[]{:S(2)}, u32[]{:S(2)}) collective-permute-start(bf16[192,768]{1,0:T(8,128)(2,1)} %refs_0_.1), channel_id=1, source_target_pairs={{0,7},{1,0},{2,1},{3,2},{4,3},{5,4},{6,5},{7,6},{8,15},{9,8},{10,9... | collective-permute-start | bytes 884744 | tf_op jit(solution)/shard_map/ppermute | solution.py:33
  8.1 31.8 %copy-start = (bf16[192,768]{1,0:T(8,128)(2,1)S(1)}, bf16[192,768]{1,0:T(8,128)(2,1)}, u32[]{:S(2)}) copy-start(bf16[192,768]{1,0:T(8,128)(2,1)} %refs_0_.1) | copy-start | bytes 884740
  8.1 29.4 %all-to-all-start = ((bf16[32,8,1536]{2,1,0:T(8,128)(2,1)}), bf16[32,8,1536]{2,1,0:T(8,128)(2,1)S(1)}, u32[]{:S(2)}, u32[]{:S(2)}) async-start(bf16[32,8,1536]{2,1,0:T(8,128)(2,1)} %broadcast_in_dim.16), calls=%async_computation | async-start | bytes 1572864 | tf_op jit(solution)/shard_map/all_to_all | solution.py:265
  16.3 9.6 %collective-permute-start.2 = (bf16[192,768]{1,0:T(8,128)(2,1)S(1)}, bf16[192,768]{1,0:T(8,128)(2,1)S(1)}, u32[]{:S(2)}, u32[]{:S(2)}) collective-permute-start(bf16[192,768]{1,0:T(8,128)(2,1)S(1)} %collective-permute-done.refs_1_), channel_id=1, source_target_pairs={{0,1},{1,2},{2,3},{3,4},{4,5},{5,6},{6,7},{7,0},{8,9},{9,10},{10,1... | collective-permute-start | bytes 884744 | tf_op jit(solution)/shard_map/ppermute | solution.py:32
  16.4 9.5 %collective-permute-start.3 = (bf16[192,768]{1,0:T(8,128)(2,1)S(1)}, bf16[192,768]{1,0:T(8,128)(2,1)S(1)}, u32[]{:S(2)}, u32[]{:S(2)}) collective-permute-start(bf16[192,768]{1,0:T(8,128)(2,1)S(1)} %collective-permute-done.1.refs_2_), channel_id=1, source_target_pairs={{0,7},{1,0},{2,1},{3,2},{4,3},{5,4},{6,5},{7,6},{8,15},{9,8},{10,9... | collective-permute-start | bytes 884744 | tf_op jit(solution)/shard_map/ppermute | solution.py:33
  25.9 8.7 %collective-permute-start.4 = (bf16[192,768]{1,0:T(8,128)(2,1)S(1)}, bf16[192,768]{1,0:T(8,128)(2,1)S(1)}, u32[]{:S(2)}, u32[]{:S(2)}) collective-permute-start(bf16[192,768]{1,0:T(8,128)(2,1)S(1)} %collective-permute-done.2.refs_3_), channel_id=1, source_target_pairs={{0,1},{1,2},{2,3},{3,4},{4,5},{5,6},{6,7},{7,0},{8,9},{9,10},{10,1... | collective-permute-start | bytes 884744 | tf_op jit(solution)/shard_map/ppermute | solution.py:32
  25.9 8.8 %collective-permute-start.5 = (bf16[192,768]{1,0:T(8,128)(2,1)S(1)}, bf16[192,768]{1,0:T(8,128)(2,1)S(1)}, u32[]{:S(2)}, u32[]{:S(2)}) collective-permute-start(bf16[192,768]{1,0:T(8,128)(2,1)S(1)} %collective-permute-done.3.refs_4_), channel_id=1, source_target_pairs={{0,7},{1,0},{2,1},{3,2},{4,3},{5,4},{6,5},{7,6},{8,15},{9,8},{10,9... | collective-permute-start | bytes 884744 | tf_op jit(solution)/shard_map/ppermute | solution.py:33
  34.6 5.3 %collective-permute-start.6 = (bf16[96,768]{1,0:T(8,128)(2,1)S(1)}, bf16[96,768]{1,0:T(8,128)(2,1)S(1)}, u32[]{:S(2)}, u32[]{:S(2)}) collective-permute-start(bf16[96,768]{1,0:T(8,128)(2,1)S(1)} %slice.8), channel_id=1, source_target_pairs={{0,1},{1,2},{2,3},{3,4},{4,5},{5,6},{6,7},{7,0},{8,9},{9,10},{10,1... | collective-permute-start | bytes 442376 | tf_op jit(solution)/shard_map/ppermute | solution.py:32
  34.7 5.2 %collective-permute-start.7 = (bf16[96,768]{1,0:T(8,128)(2,1)S(1)}, bf16[96,768]{1,0:T(8,128)(2,1)S(1)}, u32[]{:S(2)}, u32[]{:S(2)}) collective-permute-start(bf16[96,768]{1,0:T(8,128)(2,1)S(1)} %slice.9), channel_id=1, source_target_pairs={{0,7},{1,0},{2,1},{3,2},{4,3},{5,4},{6,5},{7,6},{8,15},{9,8},{10,9... | collective-permute-start | bytes 442376 | tf_op jit(solution)/shard_map/ppermute | solution.py:33
  43.5 10.1 %copy-start.1 = (s32[1,2]{1,0:T(1,128)S(1)}, s32[1,2]{1,0:T(1,128)}, u32[]{:S(2)}) copy-start(s32[1,2]{1,0:T(1,128)} %param.8) | copy-start | bytes 28
  43.5 28.6 %all-to-all-start.1 = ((bf16[32,144,128]{2,1,0:T(8,128)(2,1)}), bf16[32,144,128]{2,1,0:T(8,128)(2,1)S(1)}, u32[]{:S(2)}, u32[]{:S(2)}) async-start(bf16[32,144,128]{2,1,0:T(8,128)(2,1)} %build_query.1), calls=%async_computation.1 | async-start | bytes 2359296 | tf_op jit(solution)/shard_map/all_to_all | solution.py:267
where the time goes:
time: 113 us; the launch traced here: 112 us
  waiting for transfers between devices  33 us (29%)
  starting transfers between devices  32.9 us (29%)
  Pallas kernels  22.9 us (20%)
  blocking collectives  20.8 us (18%)
  local copies, waits for them, and re-layouts  1.73 us (2%)
    all_to_all x1, blocking collectives, per_device(): lax.all_to_all(mixed, 'wide', split_axis=0, concat_axis=0, tiled=True)  20.8 us
    all_to_all x1, waiting for transfers between devices, per_device(): lax.all_to_all(query, 'wide', split_axis=0, concat_axis=0, tiled=True)  17.7 us
    pallas_call x1, Pallas kernels, attend(): pl.pallas_call(functools.partial(attend_kernel, heads, drafts, kv, rope,...  17.1 us
    ppermute x4, waiting for transfers between devices, ring_gather(): ahead = lax.ppermute(ahead[:middle] if last else ahead, axis_name, up)  15.3 us
    ppermute x4, starting transfers between devices, ring_gather(): behind = lax.ppermute(behind[middle:] if last else behind, axis_name, down)  12 us
    all_to_all x1, starting transfers between devices, per_device(): lax.all_to_all(query, 'wide', split_axis=0, concat_axis=0, tiled=True)  10.1 us
    all_to_all x1, starting transfers between devices, per_device(): lax.all_to_all(copies, 'wide', split_axis=0, concat_axis=0, tiled=True)  8.17 us
    pallas_call x1, Pallas kernels, build_query(): pl.pallas_call(functools.partial(query_kernel, layout, heads, nope, rope,...  3.56 us
  transfers between devices with their start and end apart: 10, of which 4 were waited for; matrix products, arithmetic and copies ran while one was open for 2% of the time, Pallas kernels for 0%

commit v1 on v0

--- a/solution.py
+++ b/solution.py
@@ -11,7 +11,6 @@
 
 BF16 = jnp.bfloat16
 F32 = jnp.float32
-VMEM_LIMIT = 58 << 20
 LANES = 128
 BLOCK = 2048
 
@@ -25,17 +24,24 @@
     down = [(i, (i - 1) % size) for i in range(size)]
     half = size // 2
     middle = block.shape[0] // 2
-    ahead = behind = block
-    pieces = [((0, 0), block)]
-    for step in range(1, half + 1):
-        last = step == half
-        ahead = lax.ppermute(ahead[:middle] if last else ahead, axis_name, up)
-        behind = lax.ppermute(behind[middle:] if last else behind, axis_name, down)
-        pieces += [((size - step, 0), ahead), ((step, middle if last else 0), behind)]
+    spans = ((0, middle), (middle, block.shape[0]))
+    ahead = lax.ppermute(block, axis_name, up)
+    behind = lax.ppermute(block, axis_name, down)
+    pieces = [((0, 0), block), ((size - 1, 0), ahead), ((1, 0), behind)]
+    ahead = [ahead[first:last] for first, last in spans]
+    behind = [behind[first:last] for first, last in spans]
+    for step in range(2, half + 1):
+        for c, (first, _) in enumerate(spans):
+            if step < half or c == 0:
+                ahead[c] = lax.ppermute(ahead[c], axis_name, up)
+                pieces.append(((size - step, first), ahead[c]))
+            if step < half or c == 1:
+                behind[c] = lax.ppermute(behind[c], axis_name, down)
+                pieces.append(((step, first), behind[c]))
     return pieces
 
 
-def query_kernel(layout, heads, nope, rope, owned, me_ref, q_ref, absorb_ref, *refs):
+def query_kernel(layout, heads, nope, rope, owned, me_ref, cos_ref, sin_ref, q_ref, absorb_ref, *refs):
     *piece_refs, out_ref, w_ref, stage_ref = refs
     me = me_ref[0]
     senders, local_rows, depth = q_ref.shape
@@ -72,7 +78,7 @@
     out_ref[:, parts * each :, :] = jnp.where(lane < rope, tails[:, 0], tails[:, 1]).astype(BF16)
 
 
-def build_query(me, q_all, pieces, absorb, rope, owned):
+def build_query(me, early, q_all, pieces, absorb, rope, owned):
     layout = tuple(place for place, _ in pieces)
     flat = [piece for _, piece in pieces]
     heads, nope, kv = absorb.shape
@@ -82,16 +88,17 @@
     out_rows = local_rows * heads * (kv + rope) // LANES
     return pl.pallas_call(
         functools.partial(query_kernel, layout, heads, nope, rope, owned),
-        out_shape=jax.ShapeDtypeStruct((senders, out_rows, LANES), BF16),
-        in_specs=[pl.BlockSpec(memory_space=pltpu.SMEM)] + [vmem] * (2 + len(flat)),
+        out_shape=pltpu.VMEM((senders, out_rows, LANES), BF16),
+        in_specs=[pl.BlockSpec(memory_space=pltpu.SMEM)]
+        + [vmem] * (len(early) + 2 + len(flat)),
         out_specs=vmem,
         scratch_shapes=[
             pltpu.VMEM((depth, flat[0].shape[1]), BF16),
             pltpu.VMEM((kv // LANES + 1, rows * heads, LANES), F32),
         ],
-        compiler_params=pltpu.CompilerParams(vmem_limit_bytes=VMEM_LIMIT),
+        compiler_params=pltpu.CompilerParams(vmem_limit_bytes=24 << 20),
         name="build_query",
-    )(me, near(q_all), absorb, *[near(piece) for piece in flat])
+    )(me, *[near(table) for table in early], near(q_all), absorb, *[near(piece) for piece in flat])
 
 
 def attend_kernel(heads, drafts, kv, rope, factor, len_ref, q_ref, cos_ref, sin_ref, cache_ref, out_ref, *scratch):
@@ -110,28 +117,30 @@
             cache_ref.at[0, r, :, span], key_ref.at[r, :, span], sem.at[r, b]
         )
 
-    limits = []
+    totals = []
     for r in range(owned):
-        length = len_ref[0, r]
-        total = jnp.minimum((length + drafts - 1) // BLOCK + 1, blocks)
-        limits.append((length, (length + 1) // BLOCK, total))
+        totals.append(jnp.minimum((len_ref[0, r] + drafts - 1) // BLOCK + 1, blocks))
         for b in range(blocks):
 
-            @pl.when(b < limits[r][2])
+            @pl.when(b < totals[r])
             def _():
                 copy_of(r, b).start()
 
     for r in range(owned):
-        length, full_blocks, total = limits[r]
         for g in range(parts):
             first = (g * owned + r) * group
-            qm_ref[:, g * LANES : (g + 1) * LANES] = q_ref[:, first : first + group, :].reshape(
+            qm_ref[r, :, g * LANES : (g + 1) * LANES] = q_ref[:, first : first + group, :].reshape(
                 rows, LANES
             )
         tail = q_ref[:, parts * owned * group :, r * rope : (r + 1) * rope].astype(F32)
         swapped = jnp.concatenate([tail[..., half:], tail[..., :half]], axis=-1)
         turned = tail * cos_ref[r] + swapped * sin_ref[r]
-        qm_ref[:, kv:] = turned.astype(BF16).reshape(rows, rope)
+        qm_ref[r, :, kv:] = turned.astype(BF16).reshape(rows, rope)
+
+    for r in range(owned):
+        length = len_ref[0, r]
+        full_blocks = (length + 1) // BLOCK
+        total = totals[r]
         peak_ref[...] = jnp.full(peak_ref.shape, -jnp.inf, F32)
         sum_ref[...] = jnp.zeros(sum_ref.shape, F32)
         acc_ref[...] = jnp.zeros(acc_ref.shape, F32)
@@ -140,8 +149,9 @@
             copy_of(r, b).wait()
             start = pl.multiple_of(b * BLOCK, BLOCK)
             scores = jnp.dot(
-                qm_ref[...], key_ref[r, :, pl.ds(start, BLOCK)], preferred_element_type=F32
+                qm_ref[r], key_ref[r, :, pl.ds(start, BLOCK)], preferred_element_type=F32
             )
+            scores = scores * factor
             if masked:
                 slot = start + lax.broadcasted_iota(jnp.int32, scores.shape, 1)
                 row = lax.broadcasted_iota(jnp.int32, scores.shape, 0)
@@ -163,11 +173,11 @@
 
         lax.fori_loop(0, full_blocks, plain, 0)
         lax.fori_loop(full_blocks, total, edge, 0)
-        peak = jnp.max(peak_ref[...], axis=1, keepdims=True) * factor
+        peak = jnp.max(peak_ref[...], axis=1, keepdims=True)
 
         def mix_block(b, carry):
             start = pl.multiple_of(b * BLOCK, BLOCK)
-            weights = jnp.exp2(score_ref[:, pl.ds(start, BLOCK)] * factor - peak)
+            weights = jnp.exp2(score_ref[:, pl.ds(start, BLOCK)] - peak)
             partial = sum_ref[...]
             for g in range(BLOCK // LANES):
                 partial = partial + weights[:, g * LANES : (g + 1) * LANES]
@@ -195,27 +205,23 @@
     vmem = pl.BlockSpec(memory_space=pltpu.VMEM)
     return pl.pallas_call(
         functools.partial(attend_kernel, heads, drafts, kv, rope, scale * math.log2(math.e)),
-        out_shape=jax.ShapeDtypeStruct((senders, owned * group, kv), BF16),
-        in_specs=[
-            pl.BlockSpec(memory_space=pltpu.SMEM),
-            vmem,
-            vmem,
-            vmem,
-            pl.BlockSpec(memory_space=pl.ANY),
-        ],
+        out_shape=pltpu.VMEM((senders, owned * group, kv), BF16),
+        in_specs=[pl.BlockSpec(memory_space=pltpu.SMEM)]
+        + [vmem] * 3
+        + [pl.BlockSpec(memory_space=pl.ANY)],
         out_specs=vmem,
         scratch_shapes=[
             pltpu.VMEM((owned, width, slots), BF16),
-            pltpu.VMEM((rows, width), BF16),
+            pltpu.VMEM((owned, rows, width), BF16),
             pltpu.VMEM((rows, slots), F32),
             pltpu.VMEM((rows, LANES), F32),
             pltpu.VMEM((rows, LANES), F32),
             pltpu.VMEM((rows, kv), F32),
             pltpu.SemaphoreType.DMA((owned, slots // BLOCK)),
         ],
-        compiler_params=pltpu.CompilerParams(vmem_limit_bytes=VMEM_LIMIT),
+        compiler_params=pltpu.CompilerParams(vmem_limit_bytes=48 << 20),
         name="attend",
-    )(lengths, near(arrived), cosine, sine, cache)
+    )(lengths, near(arrived), near(cosine), near(sine), cache)
 
 
 def value_kernel(lat_ref, up_ref, out_ref, stage_ref):
@@ -243,9 +249,9 @@
         in_specs=[vmem, vmem],
         out_specs=vmem,
         scratch_shapes=[pltpu.VMEM((kv // LANES, rows, LANES), F32)],
-        compiler_params=pltpu.CompilerParams(vmem_limit_bytes=VMEM_LIMIT),
+        compiler_params=pltpu.CompilerParams(vmem_limit_bytes=16 << 20),
         name="expand_values",
-    )(near(latent), up)
+    )(near(latent), near(up))
 
 
 def per_device(
@@ -258,14 +264,6 @@
     _, owned, drafts, latent = q_latent.shape
     me = lax.axis_index("batch").astype(jnp.int32).reshape(1)
 
-    pieces = ring_gather(w_q_up, "batch", batch)
-    copies = jnp.broadcast_to(
-        q_latent.reshape(1, owned * drafts, latent), (wide, owned * drafts, latent)
-    )
-    q_all = lax.all_to_all(copies, "wide", split_axis=0, concat_axis=0, tiled=True)
-    query = build_query(me, q_all, pieces, w_k_absorb, rope_width, owned)
-    arrived = lax.all_to_all(query, "wide", split_axis=0, concat_axis=0, tiled=True)
-
     half = rope_width // 2
     shape = (owned, drafts * heads_here, rope_width)
     lane = lax.broadcasted_iota(jnp.int32, shape, 2)
@@ -274,6 +272,14 @@
     angles = (draft_start[0][:, None, None] + draft).astype(F32) * freqs
     cosine = jnp.cos(angles)
     sine = jnp.sin(angles) * jnp.where(lane < half, -1.0, 1.0)
+
+    pieces = ring_gather(w_q_up, "batch", batch)
+    copies = jnp.broadcast_to(
+        q_latent.reshape(1, owned * drafts, latent), (wide, owned * drafts, latent)
+    )
+    q_all = lax.all_to_all(copies, "wide", split_axis=0, concat_axis=0, tiled=True)
+    query = build_query(me, (cosine, sine), q_all, pieces, w_k_absorb, rope_width, owned)
+    arrived = lax.all_to_all(query, "wide", split_axis=0, concat_axis=0, tiled=True)
 
     mixed = attend(
         arrived,

time: 113 us -> 104 us (0.920)
  waiting for transfers between devices: 33 us -> 3.09 us
  blocking collectives: 20.8 us -> 48.7 us
  starting transfers between devices: 32.9 us -> 28.1 us
  Pallas kernels: 22.9 us -> 18.4 us
  local copies, waits for them, and re-layouts: 1.73 us -> 3.31 us
  other arithmetic: 0.78 us -> 1.92 us
    all_to_all x0 -> x1, blocking collectives: none -> 28 us  [per_device(): lax.all_to_all(query, 'wide', split_axis=0, concat_axis=0, tiled=True)]
    all_to_all x1 -> x0, waiting for transfers between devices: 17.7 us -> none  [per_device(): lax.all_to_all(query, 'wide', split_axis=0, concat_axis=0, tiled=True)]
    ppermute x8 -> x12, waiting for transfers between devices: 15.3 us -> 3.09 us  [the longest x5 3.07 us: ring_gather(): ahead[c] = lax.ppermute(ahead[c], axis_name, up)]
    all_to_all x1 -> x0, starting transfers between devices: 10.1 us -> none  [per_device(): lax.all_to_all(query, 'wide', split_axis=0, concat_axis=0, tiled=True)]
    ppermute x8 -> x12, starting transfers between devices: 14.6 us -> 20 us  [the longest x5 13.4 us: ring_gather(): behind[c] = lax.ppermute(behind[c], axis_name, down)]
    pallas_call x1, Pallas kernels: 3.56 us -> 1.49 us  [build_query(): pl.pallas_call(functools.partial(query_kernel, layout, heads, nope, rope,...]
    unnamed x4 -> x12, local copies, waits for them, and re-layouts: 0.01 us -> 1.59 us
    pallas_call x1, Pallas kernels: 17.1 us -> 15.7 us  [attend(): pl.pallas_call(functools.partial(attend_kernel, heads, drafts, kv, rope,...]
  transfers between devices with their start and end apart: 10 -> 13, of which waited for: 4 -> 2; matrix products, arithmetic and copies ran while one was open for 2% -> 4% of each run, Pallas kernels for 0% -> 0%
where the time goes in v1:
time: 104 us
  blocking collectives  48.7 us (47%)
  starting transfers between devices  28.1 us (27%)
  Pallas kernels  18.4 us (18%)
  local copies, waits for them, and re-layouts  3.31 us (3%)
  waiting for transfers between devices  3.09 us (3%)
  other arithmetic  1.92 us (2%)
    all_to_all x1, blocking collectives, per_device(): lax.all_to_all(query, 'wide', split_axis=0, concat_axis=0, tiled=True)  28 us
    all_to_all x1, blocking collectives, per_device(): lax.all_to_all(mixed, 'wide', split_axis=0, concat_axis=0, tiled=True)  20.7 us
    pallas_call x1, Pallas kernels, attend(): pl.pallas_call(functools.partial(attend_kernel, heads, drafts, kv, rope,...  15.7 us
    ppermute x5, starting transfers between devices, ring_gather(): behind[c] = lax.ppermute(behind[c], axis_name, down)  13.4 us
    all_to_all x1, starting transfers between devices, per_device(): lax.all_to_all(copies, 'wide', split_axis=0, concat_axis=0, tiled=True)  8.17 us
    ppermute x1, starting transfers between devices, ring_gather(): behind = lax.ppermute(block, axis_name, down)  3.94 us
    ppermute x5, waiting for transfers between devices, ring_gather(): ahead[c] = lax.ppermute(ahead[c], axis_name, up)  3.07 us
    ppermute x1, starting transfers between devices, ring_gather(): ahead = lax.ppermute(block, axis_name, up)  2.46 us
  transfers between devices with their start and end apart: 13, of which 2 were waited for; matrix products, arithmetic and copies ran while one was open for 4% of the time, Pallas kernels for 0%

profile of v1, /device:TPU:1, one launch (start us, length us, event | category | flops | bytes accessed | tf_op | source)
XLA Modules:
  0.0 103.7 jit_solution(14100557903611868037)
XLA Ops:
  0.0 2.5 %collective-permute-start = (bf16[192,768]{1,0:T(8,128)(2,1)}, bf16[192,768]{1,0:T(8,128)(2,1)S(1)}, u32[]{:S(2)}, u32[]{:S(2)}) collective-permute-start(bf16[192,768]{1,0:T(8,128)(2,1)} %refs_0_.1), channel_id=1, source_target_pairs={{0,1},{1,2},{2,3},{3,4},{4,5},{5,6},{6,7},{7,0},{8,9},{9,10},{10,1... | collective-permute-start | bytes 884744 | tf_op jit(solution)/shard_map/ppermute | solution.py:28
  2.5 3.9 %collective-permute-start.1 = (bf16[192,768]{1,0:T(8,128)(2,1)}, bf16[192,768]{1,0:T(8,128)(2,1)S(1)}, u32[]{:S(2)}, u32[]{:S(2)}) collective-permute-start(bf16[192,768]{1,0:T(8,128)(2,1)} %refs_0_.1), channel_id=1, source_target_pairs={{0,7},{1,0},{2,1},{3,2},{4,3},{5,4},{6,5},{7,6},{8,15},{9,8},{10,9... | collective-permute-start | bytes 884744 | tf_op jit(solution)/shard_map/ppermute | solution.py:29
  6.4 0.7 broadcast_in_dim.17
  7.1 0.9 broadcast_in_dim.18
  8.1 0.0 copy-start
  8.1 0.0 copy-start.2
  8.1 8.2 %all-to-all-start = ((bf16[32,8,1536]{2,1,0:T(8,128)(2,1)}), bf16[32,8,1536]{2,1,0:T(8,128)(2,1)S(1)}, u32[]{:S(2)}, u32[]{:S(2)}) async-start(bf16[32,8,1536]{2,1,0:T(8,128)(2,1)} %broadcast_in_dim.18), calls=%async_computation | async-start | bytes 1572864 | tf_op jit(solution)/shard_map/all_to_all | solution.py:280
  16.3 0.0 collective-permute-done.refs_1_
  16.3 0.1 collective-permute-start.2
  16.4 0.0 collective-permute-done.1.refs_2_
  16.4 2.7 %collective-permute-start.5 = (bf16[96,768]{1,0:T(8,128)(2,1)S(1)}, bf16[96,768]{1,0:T(8,128)(2,1)S(1)}, u32[]{:S(2)}, u32[]{:S(2)}) collective-permute-start(bf16[96,768]{1,0:T(8,128)(2,1)S(1)} %get-tuple-element.5), channel_id=1, source_target_pairs={{0,7},{1,0},{2,1},{3,2},{4,3},{5,4},{6,5},{7,6},{8,15},{9,8},{10,9... | collective-permute-start | bytes 442376 | tf_op jit(solution)/shard_map/ppermute | solution.py:39
  19.2 0.5 iota_shift-right-logical_fusion
  19.7 0.0 collective-permute-start.4
  19.7 2.7 %collective-permute-start.3 = (bf16[96,768]{1,0:T(8,128)(2,1)S(1)}, bf16[96,768]{1,0:T(8,128)(2,1)S(1)}, u32[]{:S(2)}, u32[]{:S(2)}) collective-permute-start(bf16[96,768]{1,0:T(8,128)(2,1)S(1)} %get-tuple-element.6), channel_id=1, source_target_pairs={{0,7},{1,0},{2,1},{3,2},{4,3},{5,4},{6,5},{7,6},{8,15},{9,8},{10,9... | collective-permute-start | bytes 442376 | tf_op jit(solution)/shard_map/ppermute | solution.py:39
  22.4 0.4 collective-permute-done.2.refs_3_
  22.8 0.0 collective-permute-start.6
  22.8 0.0 collective-permute-done.5.refs_6_
  22.8 2.7 %collective-permute-start.9 = (bf16[96,768]{1,0:T(8,128)(2,1)S(1)}, bf16[96,768]{1,0:T(8,128)(2,1)S(1)}, u32[]{:S(2)}, u32[]{:S(2)}) collective-permute-start(bf16[96,768]{1,0:T(8,128)(2,1)S(1)} %collective-permute-done.5.refs_6_), channel_id=1, source_target_pairs={{0,7},{1,0},{2,1},{3,2},{4,3},{5,4},{6,5},{7,6},{8,15},{9,8},{10,9... | collective-permute-start | bytes 442376 | tf_op jit(solution)/shard_map/ppermute | solution.py:39
  25.4 0.5 compare_and_fusion
  26.0 0.0 collective-permute-done.4.refs_5_
  26.0 0.1 collective-permute-start.8
  26.1 0.0 collective-permute-done.3.refs_4_
  26.1 2.7 %collective-permute-start.7 = (bf16[96,768]{1,0:T(8,128)(2,1)S(1)}, bf16[96,768]{1,0:T(8,128)(2,1)S(1)}, u32[]{:S(2)}, u32[]{:S(2)}) collective-permute-start(bf16[96,768]{1,0:T(8,128)(2,1)S(1)} %collective-permute-done.3.refs_4_), channel_id=1, source_target_pairs={{0,7},{1,0},{2,1},{3,2},{4,3},{5,4},{6,5},{7,6},{8,15},{9,8},{10,9... | collective-permute-start | bytes 442376 | tf_op jit(solution)/shard_map/ppermute | solution.py:39
  28.8 0.0 collective-permute-done.6.refs_7_
  28.8 0.0 collective-permute-start.10
  28.8 0.0 collective-permute-done.9.refs_10_
  28.8 2.7 %collective-permute-start.11 = (bf16[96,768]{1,0:T(8,128)(2,1)S(1)}, bf16[96,768]{1,0:T(8,128)(2,1)S(1)}, u32[]{:S(2)}, u32[]{:S(2)}) collective-permute-start(bf16[96,768]{1,0:T(8,128)(2,1)S(1)} %collective-permute-done.9.refs_10_), channel_id=1, source_target_pairs={{0,7},{1,0},{2,1},{3,2},{4,3},{5,4},{6,5},{7,6},{8,15},{9,8},{10,9... | collective-permute-start | bytes 442376 | tf_op jit(solution)/shard_map/ppermute | solution.py:39
  31.4 0.8 sine_multiply_fusion
  32.3 0.0 collective-permute-done.8.refs_9_
  32.3 0.0 collective-permute-done.7.refs_8_
  32.3 2.7 %collective-permute-done.10.refs_11_ = bf16[96,768]{1,0:T(8,128)(2,1)S(1)} collective-permute-done((bf16[96,768]{1,0:T(8,128)(2,1)S(1)}, bf16[96,768]{1,0:T(8,128)(2,1)S(1)}, u32[]{:S(2)}, u32[]{:S(2)}) %collective-permute-start.10) | collective-permute-done | bytes 147488 | tf_op jit(solution)/shard_map/ppermute | solution.py:36
  35.0 0.0 collective-permute-done.11.refs_12_
  35.0 0.0 copy-start.3
  35.0 0.7 copy-done.3
  35.6 0.0 all-to-all-done.q_ref
  35.6 0.0 copy-done
  35.6 0.0 copy-done.2
  35.7 0.0 copy-start.4
  35.7 0.9 copy-done.4
  36.6 1.5 %build_query.1 = bf16[32,144,128]{2,1,0:T(8,128)(2,1)S(1)} custom-call(s32[1]{0:T(128)} %bitcast.me_ref, f32[2,16,64]{2,1,0:T(8,128)S(1)} %get-tuple-element.10.cos_ref, f32[2,16,64]{2,1,0:T(8,128)S(1)} %get-tuple-element.9.sin_ref, bf16[32,8,1536]{2,1,0:T(8,128)(2,1)S(1)} %all-to-all-done.q_ref, bf16[4,128,512]{2,1,0:T(8,128)(2,1)S(1)} %copy-done, ...), custom_call_target="tpu_custom_call" | custom-call | tf_op jit(solution)/shard_map/build_query/pallas_call | solution.py:89
  38.1 0.0 copy-start.5
  38.1 28.0 %all_to_all.15.q_ref = bf16[32,144,128]{2,1,0:T(8,128)(2,1)S(1)} all-to-all(bf16[32,144,128]{2,1,0:T(8,128)(2,1)S(1)} %build_query.1), channel_id=1, replica_groups=mesh['wide'=32,'batch'=8] {'wide'}, dimensions={0} | all-to-all | bytes 2359296 | tf_op jit(solution)/shard_map/all_to_all | solution.py:282
  66.1 0.0 copy-done.5
  66.1 15.7 %attend.1 = bf16[32,32,512]{2,1,0:T(8,128)(2,1)S(1)} custom-call(s32[1,2]{1,0:T(1,128)S(1)} %copy-done.5, bf16[32,144,128]{2,1,0:T(8,128)(2,1)S(1)} %all_to_all.15.q_ref, f32[2,16,64]{2,1,0:T(8,128)S(1)} %get-tuple-element.10.cos_ref, f32[2,16,64]{2,1,0:T(8,128)S(1)} %get-tuple-element.9.sin_ref, bf16[1,2,576,4096]{3,2,1,0:T(8,128)(2,1)} %bitcast.4), custom_call_target="tpu_custom_call" | custom-call | tf_op jit(solution)/shard_map/attend/pallas_call | solution.py:206
  81.8 0.0 copy-start.1
  81.8 20.7 %all_to_all.16.lat_ref = bf16[32,32,512]{2,1,0:T(8,128)(2,1)S(1)} all-to-all(bf16[32,32,512]{2,1,0:T(8,128)(2,1)S(1)} %attend.1), channel_id=1, replica_groups=mesh['wide'=32,'batch'=8] {'wide'}, dimensions={0} | all-to-all | bytes 2097152 | tf_op jit(solution)/shard_map/all_to_all | solution.py:296
  102.5 0.0 copy-done.1
  102.5 1.2 %expand_values.1 = bf16[64,4,512]{2,1,0:T(4,128)(2,1)} custom-call(bf16[32,32,512]{2,1,0:T(8,128)(2,1)S(1)} %all_to_all.16.lat_ref, bf16[4,512,128]{2,1,0:T(8,128)(2,1)S(1)} %copy-done.1), custom_call_target="tpu_custom_call" | custom-call | tf_op jit(solution)/shard_map/expand_values/pallas_call | solution.py:246
  (3 shorter events, 0.1 us)
Async XLA Ops:
  0.0 16.3 %collective-permute-start = (bf16[192,768]{1,0:T(8,128)(2,1)}, bf16[192,768]{1,0:T(8,128)(2,1)S(1)}, u32[]{:S(2)}, u32[]{:S(2)}) collective-permute-start(bf16[192,768]{1,0:T(8,128)(2,1)} %refs_0_.1), channel_id=1, source_target_pairs={{0,1},{1,2},{2,3},{3,4},{4,5},{5,6},{6,7},{7,0},{8,9},{9,10},{10,1... | collective-permute-start | bytes 884744 | tf_op jit(solution)/shard_map/ppermute | solution.py:28
  2.5 13.9 %collective-permute-start.1 = (bf16[192,768]{1,0:T(8,128)(2,1)}, bf16[192,768]{1,0:T(8,128)(2,1)S(1)}, u32[]{:S(2)}, u32[]{:S(2)}) collective-permute-start(bf16[192,768]{1,0:T(8,128)(2,1)} %refs_0_.1), channel_id=1, source_target_pairs={{0,7},{1,0},{2,1},{3,2},{4,3},{5,4},{6,5},{7,6},{8,15},{9,8},{10,9... | collective-permute-start | bytes 884744 | tf_op jit(solution)/shard_map/ppermute | solution.py:29
  8.1 27.6 %copy-start = (bf16[4,128,512]{2,1,0:T(8,128)(2,1)S(1)}, bf16[4,128,512]{2,1,0:T(8,128)(2,1)}, u32[]{:S(2)}) copy-start(bf16[4,128,512]{2,1,0:T(8,128)(2,1)} %absorb_ref.1) | copy-start | bytes 1572868
  8.1 27.6 %copy-start.2 = (bf16[192,768]{1,0:T(8,128)(2,1)S(1)}, bf16[192,768]{1,0:T(8,128)(2,1)}, u32[]{:S(2)}) copy-start(bf16[192,768]{1,0:T(8,128)(2,1)} %refs_0_.1) | copy-start | bytes 884740
  8.1 27.6 %all-to-all-start = ((bf16[32,8,1536]{2,1,0:T(8,128)(2,1)}), bf16[32,8,1536]{2,1,0:T(8,128)(2,1)S(1)}, u32[]{:S(2)}, u32[]{:S(2)}) async-start(bf16[32,8,1536]{2,1,0:T(8,128)(2,1)} %broadcast_in_dim.18), calls=%async_computation | async-start | bytes 1572864 | tf_op jit(solution)/shard_map/all_to_all | solution.py:280
  16.3 6.5 %collective-permute-start.2 = (bf16[96,768]{1,0:T(8,128)(2,1)S(1)}, bf16[96,768]{1,0:T(8,128)(2,1)S(1)}, u32[]{:S(2)}, u32[]{:S(2)}) collective-permute-start(bf16[96,768]{1,0:T(8,128)(2,1)S(1)} %get-tuple-element.8), channel_id=1, source_target_pairs={{0,1},{1,2},{2,3},{3,4},{4,5},{5,6},{6,7},{7,0},{8,9},{9,10},{10,1... | collective-permute-start | bytes 442376 | tf_op jit(solution)/shard_map/ppermute | solution.py:36
  16.4 6.3 %collective-permute-start.5 = (bf16[96,768]{1,0:T(8,128)(2,1)S(1)}, bf16[96,768]{1,0:T(8,128)(2,1)S(1)}, u32[]{:S(2)}, u32[]{:S(2)}) collective-permute-start(bf16[96,768]{1,0:T(8,128)(2,1)S(1)} %get-tuple-element.5), channel_id=1, source_target_pairs={{0,7},{1,0},{2,1},{3,2},{4,3},{5,4},{6,5},{7,6},{8,15},{9,8},{10,9... | collective-permute-start | bytes 442376 | tf_op jit(solution)/shard_map/ppermute | solution.py:39
  19.7 6.3 %collective-permute-start.4 = (bf16[96,768]{1,0:T(8,128)(2,1)S(1)}, bf16[96,768]{1,0:T(8,128)(2,1)S(1)}, u32[]{:S(2)}, u32[]{:S(2)}) collective-permute-start(bf16[96,768]{1,0:T(8,128)(2,1)S(1)} %get-tuple-element.7), channel_id=1, source_target_pairs={{0,1},{1,2},{2,3},{3,4},{4,5},{5,6},{6,7},{7,0},{8,9},{9,10},{10,1... | collective-permute-start | bytes 442376 | tf_op jit(solution)/shard_map/ppermute | solution.py:36
  19.7 6.4 %collective-permute-start.3 = (bf16[96,768]{1,0:T(8,128)(2,1)S(1)}, bf16[96,768]{1,0:T(8,128)(2,1)S(1)}, u32[]{:S(2)}, u32[]{:S(2)}) collective-permute-start(bf16[96,768]{1,0:T(8,128)(2,1)S(1)} %get-tuple-element.6), channel_id=1, source_target_pairs={{0,7},{1,0},{2,1},{3,2},{4,3},{5,4},{6,5},{7,6},{8,15},{9,8},{10,9... | collective-permute-start | bytes 442376 | tf_op jit(solution)/shard_map/ppermute | solution.py:39
  22.8 6.0 %collective-permute-start.6 = (bf16[96,768]{1,0:T(8,128)(2,1)S(1)}, bf16[96,768]{1,0:T(8,128)(2,1)S(1)}, u32[]{:S(2)}, u32[]{:S(2)}) collective-permute-start(bf16[96,768]{1,0:T(8,128)(2,1)S(1)} %collective-permute-done.2.refs_3_), channel_id=1, source_target_pairs={{0,1},{1,2},{2,3},{3,4},{4,5},{5,6},{6,7},{7,0},{8,9},{9,10},{10,1... | collective-permute-start | bytes 442376 | tf_op jit(solution)/shard_map/ppermute | solution.py:36
  22.8 6.0 %collective-permute-start.9 = (bf16[96,768]{1,0:T(8,128)(2,1)S(1)}, bf16[96,768]{1,0:T(8,128)(2,1)S(1)}, u32[]{:S(2)}, u32[]{:S(2)}) collective-permute-start(bf16[96,768]{1,0:T(8,128)(2,1)S(1)} %collective-permute-done.5.refs_6_), channel_id=1, source_target_pairs={{0,7},{1,0},{2,1},{3,2},{4,3},{5,4},{6,5},{7,6},{8,15},{9,8},{10,9... | collective-permute-start | bytes 442376 | tf_op jit(solution)/shard_map/ppermute | solution.py:39
  26.0 6.3 %collective-permute-start.8 = (bf16[96,768]{1,0:T(8,128)(2,1)S(1)}, bf16[96,768]{1,0:T(8,128)(2,1)S(1)}, u32[]{:S(2)}, u32[]{:S(2)}) collective-permute-start(bf16[96,768]{1,0:T(8,128)(2,1)S(1)} %collective-permute-done.4.refs_5_), channel_id=1, source_target_pairs={{0,1},{1,2},{2,3},{3,4},{4,5},{5,6},{6,7},{7,0},{8,9},{9,10},{10,1... | collective-permute-start | bytes 442376 | tf_op jit(solution)/shard_map/ppermute | solution.py:36
  26.1 6.2 %collective-permute-start.7 = (bf16[96,768]{1,0:T(8,128)(2,1)S(1)}, bf16[96,768]{1,0:T(8,128)(2,1)S(1)}, u32[]{:S(2)}, u32[]{:S(2)}) collective-permute-start(bf16[96,768]{1,0:T(8,128)(2,1)S(1)} %collective-permute-done.3.refs_4_), channel_id=1, source_target_pairs={{0,7},{1,0},{2,1},{3,2},{4,3},{5,4},{6,5},{7,6},{8,15},{9,8},{10,9... | collective-permute-start | bytes 442376 | tf_op jit(solution)/shard_map/ppermute | solution.py:39
  28.8 6.2 %collective-permute-start.10 = (bf16[96,768]{1,0:T(8,128)(2,1)S(1)}, bf16[96,768]{1,0:T(8,128)(2,1)S(1)}, u32[]{:S(2)}, u32[]{:S(2)}) collective-permute-start(bf16[96,768]{1,0:T(8,128)(2,1)S(1)} %collective-permute-done.6.refs_7_), channel_id=1, source_target_pairs={{0,1},{1,2},{2,3},{3,4},{4,5},{5,6},{6,7},{7,0},{8,9},{9,10},{10,1... | collective-permute-start | bytes 442376 | tf_op jit(solution)/shard_map/ppermute | solution.py:36
  28.8 6.2 %collective-permute-start.11 = (bf16[96,768]{1,0:T(8,128)(2,1)S(1)}, bf16[96,768]{1,0:T(8,128)(2,1)S(1)}, u32[]{:S(2)}, u32[]{:S(2)}) collective-permute-start(bf16[96,768]{1,0:T(8,128)(2,1)S(1)} %collective-permute-done.9.refs_10_), channel_id=1, source_target_pairs={{0,7},{1,0},{2,1},{3,2},{4,3},{5,4},{6,5},{7,6},{8,15},{9,8},{10,9... | collective-permute-start | bytes 442376 | tf_op jit(solution)/shard_map/ppermute | solution.py:39
  35.0 0.7 copy-start.3
  35.7 0.9 copy-start.4
  38.1 28.0 %copy-start.5 = (s32[1,2]{1,0:T(1,128)S(1)}, s32[1,2]{1,0:T(1,128)}, u32[]{:S(2)}) copy-start(s32[1,2]{1,0:T(1,128)} %len_ref.1) | copy-start | bytes 28
  81.8 20.7 %copy-start.1 = (bf16[4,512,128]{2,1,0:T(8,128)(2,1)S(1)}, bf16[4,512,128]{2,1,0:T(8,128)(2,1)}, u32[]{:S(2)}) copy-start(bf16[4,512,128]{2,1,0:T(8,128)(2,1)} %up_ref.1) | copy-start | bytes 1572868

commit v2 on v1

--- a/solution.py
+++ b/solution.py
@@ -41,19 +41,50 @@
     return pieces
 
 
-def query_kernel(layout, heads, nope, rope, owned, me_ref, cos_ref, sin_ref, q_ref, absorb_ref, *refs):
-    *piece_refs, out_ref, w_ref, stage_ref = refs
+def near_part_kernel(layout, me_ref, q_ref, *refs):
+    *piece_refs, part_ref, last_ref, w_ref = refs
     me = me_ref[0]
     senders, local_rows, depth = q_ref.shape
+    size = piece_refs[0].shape[0]
+    count = depth // size
+    for (back, row), piece in zip(layout, piece_refs):
+        start = pl.multiple_of(lax.rem(me + back, count) * size + row, 32)
+        w_ref[pl.ds(start, piece.shape[0]), :] = piece[...]
+    missing = lax.rem(me + count // 2, count)
+    start = pl.multiple_of(missing * size, 64)
+    w_ref[pl.ds(start, size), :] = jnp.zeros((size, w_ref.shape[1]), BF16)
+    q = q_ref[...].reshape(senders * local_rows, depth)
+    last = q[:, :size]
+    for k in range(1, count):
+        last = jnp.where(missing == k, q[:, k * size : (k + 1) * size], last)
+    last_ref[...] = last
+    part_ref[...] = jnp.dot(q, w_ref[...], preferred_element_type=F32)
+
+
+def near_part(me, q_all, pieces):
+    senders, local_rows, depth = q_all.shape
     rows = senders * local_rows
+    size, columns = pieces[0][1].shape
+    vmem = pl.BlockSpec(memory_space=pltpu.VMEM)
+    return pl.pallas_call(
+        functools.partial(near_part_kernel, tuple(place for place, _ in pieces)),
+        out_shape=[pltpu.VMEM((rows, columns), F32), pltpu.VMEM((rows, size), BF16)],
+        in_specs=[pl.BlockSpec(memory_space=pltpu.SMEM)] + [vmem] * (1 + len(pieces)),
+        out_specs=[vmem, vmem],
+        scratch_shapes=[pltpu.VMEM((depth, columns), BF16)],
+        compiler_params=pltpu.CompilerParams(vmem_limit_bytes=16 << 20),
+        name="near_part",
+    )(me, near(q_all), *[near(piece) for _, piece in pieces])
+
+
+def query_kernel(heads, nope, rope, owned, local_rows, cos_ref, sin_ref, part_ref, last_ref, top_ref, low_ref, absorb_ref, out_ref, stage_ref):
+    rows = part_ref.shape[0]
+    senders = rows // local_rows
     width = nope + rope
     kv = absorb_ref.shape[2]
     parts = kv // LANES
-    size = piece_refs[0].shape[0]
-    for (back, row), piece in zip(layout, piece_refs):
-        start = pl.multiple_of(lax.rem(me + back, depth // size) * size + row, 32)
-        w_ref[pl.ds(start, piece.shape[0]), :] = piece[...]
-    full = jnp.dot(q_ref[...].reshape(rows, depth), w_ref[...], preferred_element_type=F32)
+    w = jnp.concatenate([top_ref[...], low_ref[...]], axis=0)
+    full = part_ref[...] + jnp.dot(last_ref[...], w, preferred_element_type=F32)
     full = full.astype(BF16).astype(F32)
     for head in range(heads):
         start = head * width
@@ -79,26 +110,21 @@
 
 
 def build_query(me, early, q_all, pieces, absorb, rope, owned):
-    layout = tuple(place for place, _ in pieces)
-    flat = [piece for _, piece in pieces]
     heads, nope, kv = absorb.shape
-    senders, local_rows, depth = q_all.shape
+    senders, local_rows, _ = q_all.shape
     rows = senders * local_rows
+    part, last = near_part(me, q_all, pieces[:-2])
     vmem = pl.BlockSpec(memory_space=pltpu.VMEM)
     out_rows = local_rows * heads * (kv + rope) // LANES
     return pl.pallas_call(
-        functools.partial(query_kernel, layout, heads, nope, rope, owned),
+        functools.partial(query_kernel, heads, nope, rope, owned, local_rows),
         out_shape=pltpu.VMEM((senders, out_rows, LANES), BF16),
-        in_specs=[pl.BlockSpec(memory_space=pltpu.SMEM)]
-        + [vmem] * (len(early) + 2 + len(flat)),
+        in_specs=[vmem] * 7,
         out_specs=vmem,
-        scratch_shapes=[
-            pltpu.VMEM((depth, flat[0].shape[1]), BF16),
-            pltpu.VMEM((kv // LANES + 1, rows * heads, LANES), F32),
-        ],
-        compiler_params=pltpu.CompilerParams(vmem_limit_bytes=24 << 20),
+        scratch_shapes=[pltpu.VMEM((kv // LANES + 1, rows * heads, LANES), F32)],
+        compiler_params=pltpu.CompilerParams(vmem_limit_bytes=16 << 20),
         name="build_query",
-    )(me, *[near(table) for table in early], near(q_all), absorb, *[near(piece) for piece in flat])
+    )(*[near(x) for x in (*early, part, last, pieces[-2][1], pieces[-1][1])], absorb)
 
 
 def attend_kernel(heads, drafts, kv, rope, factor, len_ref, q_ref, cos_ref, sin_ref, cache_ref, out_ref, *scratch):

time: 104 us -> 103 us (level)
  waiting for transfers between devices: 3.09 us -> 6.43 us
  other arithmetic: 1.92 us -> 0.17 us
  local copies, waits for them, and re-layouts: 3.31 us -> 1.75 us
    ppermute x5, waiting for transfers between devices: 3.07 us -> 5.67 us  [ring_gather(): ahead[c] = lax.ppermute(ahead[c], axis_name, up)]
    ppermute x5, starting transfers between devices: 13.4 us -> 11.5 us  [ring_gather(): behind[c] = lax.ppermute(behind[c], axis_name, down)]
    unnamed x12 -> x10, local copies, waits for them, and re-layouts: 1.59 us -> 0.02 us
  transfers between devices with their start and end apart: 13 -> 13, of which waited for: 2 -> 5; matrix products, arithmetic and copies ran while one was open for 4% -> 2% of each run, Pallas kernels for 0% -> 1%
where the time goes in v2:
time: 103 us
  blocking collectives  48.7 us (47%)
  starting transfers between devices  27.2 us (26%)
  Pallas kernels  18.6 us (18%)
  waiting for transfers between devices  6.43 us (6%)
  local copies, waits for them, and re-layouts  1.75 us (2%)
    all_to_all x1, blocking collectives, per_device(): lax.all_to_all(query, 'wide', split_axis=0, concat_axis=0, tiled=True)  28 us
    all_to_all x1, blocking collectives, per_device(): lax.all_to_all(mixed, 'wide', split_axis=0, concat_axis=0, tiled=True)  20.7 us
    pallas_call x1, Pallas kernels, attend(): pl.pallas_call(functools.partial(attend_kernel, heads, drafts, kv, rope,...  15.7 us
    ppermute x5, starting transfers between devices, ring_gather(): behind[c] = lax.ppermute(behind[c], axis_name, down)  11.5 us
    all_to_all x1, starting transfers between devices, per_device(): lax.all_to_all(copies, 'wide', split_axis=0, concat_axis=0, tiled=True)  8.17 us
    ppermute x5, waiting for transfers between devices, ring_gather(): ahead[c] = lax.ppermute(ahead[c], axis_name, up)  5.67 us
    ppermute x1, starting transfers between devices, ring_gather(): behind = lax.ppermute(block, axis_name, down)  3.94 us
    ppermute x1, starting transfers between devices, ring_gather(): ahead = lax.ppermute(block, axis_name, up)  2.46 us
  transfers between devices with their start and end apart: 13, of which 5 were waited for; matrix products, arithmetic and copies ran while one was open for 2% of the time, Pallas kernels for 1%

profile of v2, /device:TPU:1, one launch (start us, length us, event | category | flops | bytes accessed | tf_op | source)
XLA Modules:
  0.0 102.9 jit_solution(3041258125478897647)
XLA Ops:
  0.0 2.5 %collective-permute-start = (bf16[192,768]{1,0:T(8,128)(2,1)}, bf16[192,768]{1,0:T(8,128)(2,1)S(1)}, u32[]{:S(2)}, u32[]{:S(2)}) collective-permute-start(bf16[192,768]{1,0:T(8,128)(2,1)} %refs_0_.1), channel_id=1, source_target_pairs={{0,1},{1,2},{2,3},{3,4},{4,5},{5,6},{6,7},{7,0},{8,9},{9,10},{10,1... | collective-permute-start | bytes 884744 | tf_op jit(solution)/shard_map/ppermute | solution.py:28
  2.5 3.9 %collective-permute-start.1 = (bf16[192,768]{1,0:T(8,128)(2,1)}, bf16[192,768]{1,0:T(8,128)(2,1)S(1)}, u32[]{:S(2)}, u32[]{:S(2)}) collective-permute-start(bf16[192,768]{1,0:T(8,128)(2,1)} %refs_0_.1), channel_id=1, source_target_pairs={{0,7},{1,0},{2,1},{3,2},{4,3},{5,4},{6,5},{7,6},{8,15},{9,8},{10,9... | collective-permute-start | bytes 884744 | tf_op jit(solution)/shard_map/ppermute | solution.py:29
  6.4 0.7 broadcast_in_dim.17
  7.1 0.9 broadcast_in_dim.18
  8.1 0.0 copy-start.4
  8.1 0.0 copy-start.2
  8.1 8.2 %all-to-all-start = ((bf16[32,8,1536]{2,1,0:T(8,128)(2,1)}), bf16[32,8,1536]{2,1,0:T(8,128)(2,1)S(1)}, u32[]{:S(2)}, u32[]{:S(2)}) async-start(bf16[32,8,1536]{2,1,0:T(8,128)(2,1)} %broadcast_in_dim.18), calls=%async_computation | async-start | bytes 1572864 | tf_op jit(solution)/shard_map/all_to_all | solution.py:306
  16.3 0.0 collective-permute-done.refs_1_
  16.3 0.1 collective-permute-start.2
  16.4 0.0 collective-permute-done.1.refs_2_
  16.4 2.7 %collective-permute-start.5 = (bf16[96,768]{1,0:T(8,128)(2,1)S(1)}, bf16[96,768]{1,0:T(8,128)(2,1)S(1)}, u32[]{:S(2)}, u32[]{:S(2)}) collective-permute-start(bf16[96,768]{1,0:T(8,128)(2,1)S(1)} %get-tuple-element.9), channel_id=1, source_target_pairs={{0,7},{1,0},{2,1},{3,2},{4,3},{5,4},{6,5},{7,6},{8,15},{9,8},{10,9... | collective-permute-start | bytes 442376 | tf_op jit(solution)/shard_map/ppermute | solution.py:39
  19.2 0.5 collective-permute-start.3
  19.7 0.9 collective-permute-start.4
  20.6 2.1 %collective-permute-done.2.refs_3_ = bf16[96,768]{1,0:T(8,128)(2,1)S(1)} collective-permute-done((bf16[96,768]{1,0:T(8,128)(2,1)S(1)}, bf16[96,768]{1,0:T(8,128)(2,1)S(1)}, u32[]{:S(2)}, u32[]{:S(2)}) %collective-permute-start.2) | collective-permute-done | bytes 147488 | tf_op jit(solution)/shard_map/ppermute | solution.py:36
  22.8 0.0 collective-permute-start.6
  22.8 0.0 collective-permute-done.5.refs_6_
  22.8 2.7 %collective-permute-start.9 = (bf16[96,768]{1,0:T(8,128)(2,1)S(1)}, bf16[96,768]{1,0:T(8,128)(2,1)S(1)}, u32[]{:S(2)}, u32[]{:S(2)}) collective-permute-start(bf16[96,768]{1,0:T(8,128)(2,1)S(1)} %collective-permute-done.5.refs_6_), channel_id=1, source_target_pairs={{0,7},{1,0},{2,1},{3,2},{4,3},{5,4},{6,5},{7,6},{8,15},{9,8},{10,9... | collective-permute-start | bytes 442376 | tf_op jit(solution)/shard_map/ppermute | solution.py:39
  25.5 0.0 collective-permute-done.3.refs_4_
  25.5 3.0 %collective-permute-start.7 = (bf16[96,768]{1,0:T(8,128)(2,1)S(1)}, bf16[96,768]{1,0:T(8,128)(2,1)S(1)}, u32[]{:S(2)}, u32[]{:S(2)}) collective-permute-start(bf16[96,768]{1,0:T(8,128)(2,1)S(1)} %collective-permute-done.3.refs_4_), channel_id=1, source_target_pairs={{0,7},{1,0},{2,1},{3,2},{4,3},{5,4},{6,5},{7,6},{8,15},{9,8},{10,9... | collective-permute-start | bytes 442376 | tf_op jit(solution)/shard_map/ppermute | solution.py:39
  28.4 0.0 collective-permute-done.4.refs_5_
  28.4 0.0 collective-permute-start.8
  28.4 0.1 collective-permute-done.6.refs_7_
  28.5 0.1 collective-permute-start.10
  28.6 0.0 collective-permute-done.9.refs_10_
  28.6 2.6 %collective-permute-start.11 = (bf16[96,768]{1,0:T(8,128)(2,1)S(1)}, bf16[96,768]{1,0:T(8,128)(2,1)S(1)}, u32[]{:S(2)}, u32[]{:S(2)}) collective-permute-start(bf16[96,768]{1,0:T(8,128)(2,1)S(1)} %collective-permute-done.9.refs_10_), channel_id=1, source_target_pairs={{0,7},{1,0},{2,1},{3,2},{4,3},{5,4},{6,5},{7,6},{8,15},{9,8},{10,9... | collective-permute-start | bytes 442376 | tf_op jit(solution)/shard_map/ppermute | solution.py:39
  31.2 0.0 copy-done.4
  31.2 0.1 sine_multiply_fusion
  31.4 0.7 collective-permute-done.7.refs_8_
  32.1 1.5 %collective-permute-done.8.refs_9_ = bf16[96,768]{1,0:T(8,128)(2,1)S(1)} collective-permute-done((bf16[96,768]{1,0:T(8,128)(2,1)S(1)}, bf16[96,768]{1,0:T(8,128)(2,1)S(1)}, u32[]{:S(2)}, u32[]{:S(2)}) %collective-permute-start.8) | collective-permute-done | bytes 147488 | tf_op jit(solution)/shard_map/ppermute | solution.py:36
  33.6 0.0 all-to-all-done.q_ref
  33.6 0.0 copy-done.2
  33.6 0.0 copy-start.1
  33.6 0.9 near_part.1
  34.6 1.9 %collective-permute-done.10.top_ref = bf16[96,768]{1,0:T(8,128)(2,1)S(1)} collective-permute-done((bf16[96,768]{1,0:T(8,128)(2,1)S(1)}, bf16[96,768]{1,0:T(8,128)(2,1)S(1)}, u32[]{:S(2)}, u32[]{:S(2)}) %collective-permute-start.10) | collective-permute-done | bytes 147488 | tf_op jit(solution)/shard_map/ppermute | solution.py:36
  36.5 0.0 collective-permute-done.11.low_ref
  36.5 0.0 copy-done.1
  36.5 0.8 build_query.1
  37.3 0.0 copy-start.3
  37.3 28.0 %all_to_all.15.q_ref = bf16[32,144,128]{2,1,0:T(8,128)(2,1)S(1)} all-to-all(bf16[32,144,128]{2,1,0:T(8,128)(2,1)S(1)} %build_query.1), channel_id=1, replica_groups=mesh['wide'=32,'batch'=8] {'wide'}, dimensions={0} | all-to-all | bytes 2359296 | tf_op jit(solution)/shard_map/all_to_all | solution.py:308
  65.3 0.0 copy-done.3
  65.3 15.7 %attend.1 = bf16[32,32,512]{2,1,0:T(8,128)(2,1)S(1)} custom-call(s32[1,2]{1,0:T(1,128)S(1)} %copy-done.3, bf16[32,144,128]{2,1,0:T(8,128)(2,1)S(1)} %all_to_all.15.q_ref, f32[2,16,64]{2,1,0:T(8,128)S(1)} %get-tuple-element.14.cos_ref, f32[2,16,64]{2,1,0:T(8,128)S(1)} %get-tuple-element.13.sin_ref, bf16[1,2,576,4096]{3,2,1,0:T(8,128)(2,1)} %bitcast.4), custom_call_target="tpu_custom_call" | custom-call | tf_op jit(solution)/shard_map/attend/pallas_call | solution.py:232
  81.0 0.0 copy-start
  81.0 20.7 %all_to_all.16.lat_ref = bf16[32,32,512]{2,1,0:T(8,128)(2,1)S(1)} all-to-all(bf16[32,32,512]{2,1,0:T(8,128)(2,1)S(1)} %attend.1), channel_id=1, replica_groups=mesh['wide'=32,'batch'=8] {'wide'}, dimensions={0} | all-to-all | bytes 2097152 | tf_op jit(solution)/shard_map/all_to_all | solution.py:322
  101.7 0.0 copy-done
  101.7 1.2 %expand_values.1 = bf16[64,4,512]{2,1,0:T(4,128)(2,1)} custom-call(bf16[32,32,512]{2,1,0:T(8,128)(2,1)S(1)} %all_to_all.16.lat_ref, bf16[4,512,128]{2,1,0:T(8,128)(2,1)S(1)} %copy-done), custom_call_target="tpu_custom_call" | custom-call | tf_op jit(solution)/shard_map/expand_values/pallas_call | solution.py:272
  (5 shorter events, 0.1 us)
Async XLA Ops:
  0.0 16.3 %collective-permute-start = (bf16[192,768]{1,0:T(8,128)(2,1)}, bf16[192,768]{1,0:T(8,128)(2,1)S(1)}, u32[]{:S(2)}, u32[]{:S(2)}) collective-permute-start(bf16[192,768]{1,0:T(8,128)(2,1)} %refs_0_.1), channel_id=1, source_target_pairs={{0,1},{1,2},{2,3},{3,4},{4,5},{5,6},{6,7},{7,0},{8,9},{9,10},{10,1... | collective-permute-start | bytes 884744 | tf_op jit(solution)/shard_map/ppermute | solution.py:28
  2.5 13.9 %collective-permute-start.1 = (bf16[192,768]{1,0:T(8,128)(2,1)}, bf16[192,768]{1,0:T(8,128)(2,1)S(1)}, u32[]{:S(2)}, u32[]{:S(2)}) collective-permute-start(bf16[192,768]{1,0:T(8,128)(2,1)} %refs_0_.1), channel_id=1, source_target_pairs={{0,7},{1,0},{2,1},{3,2},{4,3},{5,4},{6,5},{7,6},{8,15},{9,8},{10,9... | collective-permute-start | bytes 884744 | tf_op jit(solution)/shard_map/ppermute | solution.py:29
  8.1 23.1 %copy-start.4 = (s32[1,2]{1,0:T(1,128)S(1)}, s32[1,2]{1,0:T(1,128)}, u32[]{:S(2)}) copy-start(s32[1,2]{1,0:T(1,128)} %param.8) | copy-start | bytes 28
  8.1 25.6 %copy-start.2 = (bf16[192,768]{1,0:T(8,128)(2,1)S(1)}, bf16[192,768]{1,0:T(8,128)(2,1)}, u32[]{:S(2)}) copy-start(bf16[192,768]{1,0:T(8,128)(2,1)} %refs_0_.1) | copy-start | bytes 884740
  8.1 25.6 %all-to-all-start = ((bf16[32,8,1536]{2,1,0:T(8,128)(2,1)}), bf16[32,8,1536]{2,1,0:T(8,128)(2,1)S(1)}, u32[]{:S(2)}, u32[]{:S(2)}) async-start(bf16[32,8,1536]{2,1,0:T(8,128)(2,1)} %broadcast_in_dim.18), calls=%async_computation | async-start | bytes 1572864 | tf_op jit(solution)/shard_map/all_to_all | solution.py:306
  16.3 6.5 %collective-permute-start.2 = (bf16[96,768]{1,0:T(8,128)(2,1)S(1)}, bf16[96,768]{1,0:T(8,128)(2,1)S(1)}, u32[]{:S(2)}, u32[]{:S(2)}) collective-permute-start(bf16[96,768]{1,0:T(8,128)(2,1)S(1)} %get-tuple-element.12), channel_id=1, source_target_pairs={{0,1},{1,2},{2,3},{3,4},{4,5},{5,6},{6,7},{7,0},{8,9},{9,10},{10,1... | collective-permute-start | bytes 442376 | tf_op jit(solution)/shard_map/ppermute | solution.py:36
  16.4 6.3 %collective-permute-start.5 = (bf16[96,768]{1,0:T(8,128)(2,1)S(1)}, bf16[96,768]{1,0:T(8,128)(2,1)S(1)}, u32[]{:S(2)}, u32[]{:S(2)}) collective-permute-start(bf16[96,768]{1,0:T(8,128)(2,1)S(1)} %get-tuple-element.9), channel_id=1, source_target_pairs={{0,7},{1,0},{2,1},{3,2},{4,3},{5,4},{6,5},{7,6},{8,15},{9,8},{10,9... | collective-permute-start | bytes 442376 | tf_op jit(solution)/shard_map/ppermute | solution.py:39
  19.2 6.3 %collective-permute-start.3 = (bf16[96,768]{1,0:T(8,128)(2,1)S(1)}, bf16[96,768]{1,0:T(8,128)(2,1)S(1)}, u32[]{:S(2)}, u32[]{:S(2)}) collective-permute-start(bf16[96,768]{1,0:T(8,128)(2,1)S(1)} %get-tuple-element.10), channel_id=1, source_target_pairs={{0,7},{1,0},{2,1},{3,2},{4,3},{5,4},{6,5},{7,6},{8,15},{9,8},{10,9... | collective-permute-start | bytes 442376 | tf_op jit(solution)/shard_map/ppermute | solution.py:39
  19.7 8.7 %collective-permute-start.4 = (bf16[96,768]{1,0:T(8,128)(2,1)S(1)}, bf16[96,768]{1,0:T(8,128)(2,1)S(1)}, u32[]{:S(2)}, u32[]{:S(2)}) collective-permute-start(bf16[96,768]{1,0:T(8,128)(2,1)S(1)} %get-tuple-element.11), channel_id=1, source_target_pairs={{0,1},{1,2},{2,3},{3,4},{4,5},{5,6},{6,7},{7,0},{8,9},{9,10},{10,1... | collective-permute-start | bytes 442376 | tf_op jit(solution)/shard_map/ppermute | solution.py:36
  22.8 5.7 %collective-permute-start.6 = (bf16[96,768]{1,0:T(8,128)(2,1)S(1)}, bf16[96,768]{1,0:T(8,128)(2,1)S(1)}, u32[]{:S(2)}, u32[]{:S(2)}) collective-permute-start(bf16[96,768]{1,0:T(8,128)(2,1)S(1)} %collective-permute-done.2.refs_3_), channel_id=1, source_target_pairs={{0,1},{1,2},{2,3},{3,4},{4,5},{5,6},{6,7},{7,0},{8,9},{9,10},{10,1... | collective-permute-start | bytes 442376 | tf_op jit(solution)/shard_map/ppermute | solution.py:36
  22.8 5.9 %collective-permute-start.9 = (bf16[96,768]{1,0:T(8,128)(2,1)S(1)}, bf16[96,768]{1,0:T(8,128)(2,1)S(1)}, u32[]{:S(2)}, u32[]{:S(2)}) collective-permute-start(bf16[96,768]{1,0:T(8,128)(2,1)S(1)} %collective-permute-done.5.refs_6_), channel_id=1, source_target_pairs={{0,7},{1,0},{2,1},{3,2},{4,3},{5,4},{6,5},{7,6},{8,15},{9,8},{10,9... | collective-permute-start | bytes 442376 | tf_op jit(solution)/shard_map/ppermute | solution.py:39
  25.5 6.6 %collective-permute-start.7 = (bf16[96,768]{1,0:T(8,128)(2,1)S(1)}, bf16[96,768]{1,0:T(8,128)(2,1)S(1)}, u32[]{:S(2)}, u32[]{:S(2)}) collective-permute-start(bf16[96,768]{1,0:T(8,128)(2,1)S(1)} %collective-permute-done.3.refs_4_), channel_id=1, source_target_pairs={{0,7},{1,0},{2,1},{3,2},{4,3},{5,4},{6,5},{7,6},{8,15},{9,8},{10,9... | collective-permute-start | bytes 442376 | tf_op jit(solution)/shard_map/ppermute | solution.py:39
  28.4 5.2 %collective-permute-start.8 = (bf16[96,768]{1,0:T(8,128)(2,1)S(1)}, bf16[96,768]{1,0:T(8,128)(2,1)S(1)}, u32[]{:S(2)}, u32[]{:S(2)}) collective-permute-start(bf16[96,768]{1,0:T(8,128)(2,1)S(1)} %collective-permute-done.4.refs_5_), channel_id=1, source_target_pairs={{0,1},{1,2},{2,3},{3,4},{4,5},{5,6},{6,7},{7,0},{8,9},{9,10},{10,1... | collective-permute-start | bytes 442376 | tf_op jit(solution)/shard_map/ppermute | solution.py:36
  28.5 8.0 %collective-permute-start.10 = (bf16[96,768]{1,0:T(8,128)(2,1)S(1)}, bf16[96,768]{1,0:T(8,128)(2,1)S(1)}, u32[]{:S(2)}, u32[]{:S(2)}) collective-permute-start(bf16[96,768]{1,0:T(8,128)(2,1)S(1)} %collective-permute-done.6.refs_7_), channel_id=1, source_target_pairs={{0,1},{1,2},{2,3},{3,4},{4,5},{5,6},{6,7},{7,0},{8,9},{9,10},{10,1... | collective-permute-start | bytes 442376 | tf_op jit(solution)/shard_map/ppermute | solution.py:36
  28.6 7.9 %collective-permute-start.11 = (bf16[96,768]{1,0:T(8,128)(2,1)S(1)}, bf16[96,768]{1,0:T(8,128)(2,1)S(1)}, u32[]{:S(2)}, u32[]{:S(2)}) collective-permute-start(bf16[96,768]{1,0:T(8,128)(2,1)S(1)} %collective-permute-done.9.refs_10_), channel_id=1, source_target_pairs={{0,7},{1,0},{2,1},{3,2},{4,3},{5,4},{6,5},{7,6},{8,15},{9,8},{10,9... | collective-permute-start | bytes 442376 | tf_op jit(solution)/shard_map/ppermute | solution.py:39
  33.6 2.9 %copy-start.1 = (bf16[4,128,512]{2,1,0:T(8,128)(2,1)S(1)}, bf16[4,128,512]{2,1,0:T(8,128)(2,1)}, u32[]{:S(2)}) copy-start(bf16[4,128,512]{2,1,0:T(8,128)(2,1)} %absorb_ref.1) | copy-start | bytes 1572868
  37.3 28.0 %copy-start.3 = (s32[1,2]{1,0:T(1,128)S(1)}, s32[1,2]{1,0:T(1,128)}, u32[]{:S(2)}) copy-start(s32[1,2]{1,0:T(1,128)} %len_ref.1) | copy-start | bytes 28
  81.0 20.7 %copy-start = (bf16[4,512,128]{2,1,0:T(8,128)(2,1)S(1)}, bf16[4,512,128]{2,1,0:T(8,128)(2,1)}, u32[]{:S(2)}) copy-start(bf16[4,512,128]{2,1,0:T(8,128)(2,1)} %up_ref.1) | copy-start | bytes 1572868
